TPU v7x, 32 devices: a whole 2x2x4 slice. The times are simulated.
32 devices in a mesh: groups: 2 (over y), tensor: 4 (over z), dp: 4 (over x, core).
Axes of the slice: x: 2, y: 2, z: 4, core: 2. Of those that a mesh axis runs over, the one named last changes fastest.
Arguments:
- out_grad: bfloat16 [4, 1280, 4096], P('dp', ('groups', 'tensor')), parts along dimension 1, may hold values from -6 to 6
- gate_pre: bfloat16 [4, 1280, 14336], P('dp', 'groups', 'tensor'), parts along dimension 1, may hold values from -8 to 8
- up_pre: bfloat16 [4, 1280, 14336], P('dp', 'groups', 'tensor'), parts along dimension 1, may hold values from -6 to 6
- down_weight: bfloat16 [14336, 4096], P('tensor'), may hold values from -0.046875 to 0.046875
Outputs:
- gate_grad: bfloat16 [4, 1280, 14336], P('dp', 'groups', 'tensor'), parts along dimension 1
- up_grad: bfloat16 [4, 1280, 14336], P('dp', 'groups', 'tensor'), parts along dimension 1
- down_grad: bfloat16 [28672, 4096], P(('groups', 'tensor'), 'dp'), parts along dimension 0
There are 2 independent parts, one for each index of `groups`. A program takes and returns all parts, laid end to end along the dimension named above; an argument that names none is the same for every part. Nothing has to cross between parts.
All inputs are finite; a program needn't handle non-finite values.
Results may differ from a plain program's by a relative error of at most 0.014.
Values may be sent and summed in bfloat16 or wider, within the bound.
A program may use at most 128 MiB of HBM per device.

v0:
```python
import math
import jax
import jax.numpy as jnp
from jax import lax
from jax.sharding import PartitionSpec as P


def on_device(out_grad, gate_pre, up_pre, down_weight):
    gate = gate_pre[0].astype(jnp.float32)
    up = up_pre[0].astype(jnp.float32)
    sig = jax.nn.sigmoid(gate)
    act = gate * sig
    hidden = (act * up).astype(jnp.bfloat16)
    scale = 1.0 / math.sqrt(hidden.shape[0] * lax.axis_size("dp"))
    hidden_all = lax.all_gather(hidden, "dp", axis=0, tiled=True)
    block = lax.all_gather(out_grad, "tensor", axis=1, tiled=True)[0]
    columns = lax.all_to_all(block, "dp", split_axis=1, concat_axis=0, tiled=True)
    hidden_grad = lax.dot_general(
        block, down_weight, (((1,), (1,)), ((), ())), preferred_element_type=jnp.float32
    )
    gate_grad = (hidden_grad * up * sig * (1.0 + gate * (1.0 - sig))).astype(jnp.bfloat16)
    up_grad = (hidden_grad * act).astype(jnp.bfloat16)
    total = jnp.einsum("tf,td->fd", hidden_all, columns, preferred_element_type=jnp.float32)
    down_grad = (total * scale).astype(jnp.bfloat16)
    return (gate_grad[None], up_grad[None], down_grad)


def solution(mesh):
    return jax.shard_map(
        on_device,
        mesh=mesh,
        in_specs=(
            P("dp", ("groups", "tensor"), None),
            P("dp", "groups", "tensor"),
            P("dp", "groups", "tensor"),
            P("tensor", None),
        ),
        out_specs=(
            P("dp", "groups", "tensor"),
            P("dp", "groups", "tensor"),
            P(("groups", "tensor"), "dp"),
        ),
        check_vma=False,
    )
```

profile of v0, /device:TPU:0, one launch (start us, length us, event | category | flops | bytes accessed | tf_op | source)
XLA Modules:
  0.0 347.5 jit_solution(11023457217963688195)
XLA Ops:
  7.2 0.0 all-gather.3.cloned.1.call-start
  7.2 0.7 all-gather.3.cloned.1.call-update
  7.9 0.0 all-gather.5.cloned.1.call-start
  7.9 102.4 %all-gather.3.cloned.1.call-done = bf16[1,640,4096]{2,1,0:T(8,128)(2,1)} async-done(((bf16[1,160,4096]{2,1,0:T(8,128)(2,1)}), bf16[1,640,4096]{2,1,0:T(8,128)(2,1)}) %all-gather.3.cloned.1.call-update) | async-done | bytes 5242896 | tf_op jit(solution)/shard_map/all_gather | solution.py:16
  110.4 33.4 %fusion.10 = (bf16[1,640,3584]{2,1,0:T(8,128)(2,1)}, bf16[1,640,3584]{2,1,0:T(8,128)(2,1)}, bf16[640,3584]{1,0:T(8,128)(2,1)}) fusion(bf16[1,640,3584]{2,1,0:T(8,128)(2,1)} %param.5, bf16[1,640,3584]{2,1,0:T(8,128)(2,1)} %param.6, bf16[3584,4096]{1,0:T(8,128)(2,1)} %param.7, bf16[1,640,4096]{2,1,0:T(8,128)(2,1)} %all-gather.3.cloned.1.call-done), kind=kOutput, calls=%fused_computation.17 | convolution fusion | flops 18829475840 | bytes 57540608 | tf_op jit(solution)/shard_map/dot_general | solution.py:18
  143.8 0.0 all-gather.5.cloned.1.call-update
  143.8 8.1 %copy.9 = bf16[1,640,4096]{1,2,0:T(8,128)(2,1)} copy(bf16[1,640,4096]{2,1,0:T(8,128)(2,1)} %all-gather.3.cloned.1.call-done) | data formatting | bytes 10485760 | tf_op jit(solution)/shard_map/all_gather | solution.py:16
  151.9 122.0 %all_to_all.19 = bf16[640,4,1024]{0,2,1:T(8,128)(2,1)} all-to-all(bf16[640,4,1024]{0,2,1:T(8,128)(2,1)} %bitcast.31), channel_id=1, replica_groups=mesh['groups'=2,'tensor'=4,'dp'=4] {'dp'}, dimensions={1} | all-to-all | bytes 10485760 | tf_op jit(solution)/shard_map/all_to_all | solution.py:17
  274.0 8.0 %copy.10 = bf16[4,640,1024]{2,1,0:T(8,128)(2,1)} copy(bf16[4,640,1024]{1,2,0:T(8,128)(2,1)} %bitcast.32) | data formatting | bytes 10485760 | tf_op jit(solution)/shard_map/all_to_all | solution.py:17
  282.0 33.6 %all-gather.5.cloned.1.call-done = bf16[2560,3584]{1,0:T(8,128)(2,1)} async-done(((bf16[640,3584]{1,0:T(8,128)(2,1)}), bf16[2560,3584]{1,0:T(8,128)(2,1)}) %all-gather.5.cloned.1.call-update) | async-done | bytes 18350096 | tf_op jit(solution)/shard_map/all_gather | solution.py:15
  315.6 25.0 %multiply_convert_fusion = bf16[3584,1024]{1,0:T(8,128)(2,1)} fusion(bf16[2560,3584]{1,0:T(8,128)(2,1)} %all-gather.5.cloned.1.call-done, bf16[2560,1024]{1,0:T(8,128)(2,1)} %bitcast.33), kind=kOutput, calls=%fused_computation | convolution fusion | flops 18797821952 | bytes 30932992 | tf_op jit(solution)/shard_map/tf,td->fd/dot_general | solution.py:23
Async XLA Ops:
  7.2 103.2 %all-gather.3.cloned.1.call-start = ((), (), s32[]{:S(2)}) async-start(), calls=%async_computation.1 | async-start | bytes 6553600 | tf_op jit(solution)/shard_map/all_gather | solution.py:16
  7.9 307.7 %all-gather.5.cloned.1.call-start = ((), (), s32[]{:S(2)}) async-start(), calls=%async_computation.2 | async-start | bytes 22937600 | tf_op jit(solution)/shard_map/all_gather | solution.py:15
Sparse Core Ops, SparseCore 0:
  9.6 100.7 all-gather.2
  143.9 171.6 all-gather.4
where the time goes:
time: 348 us; the launch traced here: 347 us
  waiting for transfers between devices  137 us (39%)
  blocking collectives  122 us (35%)
  matrix products  58.4 us (17%)
  local copies, waits for them, and re-layouts  16.2 us (5%)
  between operations  14 us (4%)
    all_to_all x1, blocking collectives, on_device(): lax.all_to_all(block, 'dp', split_axis=1, concat_axis=0, tiled=True)  122 us
    all_gather x1, waiting for transfers between devices, on_device(): block = lax.all_gather(out_grad, 'tensor', axis=1, tiled=True)[0]  102 us
    all_gather x1, waiting for transfers between devices, on_device(): hidden_all = lax.all_gather(hidden, 'dp', axis=0, tiled=True)  33.6 us
    dot_general x1, matrix products, on_device(): lax.dot_general(block, down_weight, (((1,), (1,)), ((), ())), preferred_e...  33.4 us
    dot_general x1, matrix products, on_device(): jnp.einsum('tf,td->fd', hidden_all, columns, preferred_element_type=jnp.f...  25 us
    all_gather x1, local copies, waits for them, and re-layouts, on_device(): block = lax.all_gather(out_grad, 'tensor', axis=1, tiled=True)[0]  8.13 us
    all_to_all x1, local copies, waits for them, and re-layouts, on_device(): lax.all_to_all(block, 'dp', split_axis=1, concat_axis=0, tiled=True)  8.05 us
  transfers between devices with their start and end apart: 2, of which 2 were waited for; matrix products, arithmetic and copies ran while one was open for 5% of the time, Pallas kernels for 0%

commit v1 on v0

--- a/solution.py
+++ b/solution.py
@@ -12,7 +12,6 @@
     act = gate * sig
     hidden = (act * up).astype(jnp.bfloat16)
     scale = 1.0 / math.sqrt(hidden.shape[0] * lax.axis_size("dp"))
-    hidden_all = lax.all_gather(hidden, "dp", axis=0, tiled=True)
     block = lax.all_gather(out_grad, "tensor", axis=1, tiled=True)[0]
     columns = lax.all_to_all(block, "dp", split_axis=1, concat_axis=0, tiled=True)
     hidden_grad = lax.dot_general(
@@ -20,7 +19,20 @@
     )
     gate_grad = (hidden_grad * up * sig * (1.0 + gate * (1.0 - sig))).astype(jnp.bfloat16)
     up_grad = (hidden_grad * act).astype(jnp.bfloat16)
-    total = jnp.einsum("tf,td->fd", hidden_all, columns, preferred_element_type=jnp.float32)
+    size, index, rows = (lax.axis_size("dp"), lax.axis_index("dp"), hidden.shape[0])
+    right = [(i, (i + 1) % size) for i in range(size)]
+    held, total_2 = (hidden, None)
+    for step in range(size):
+        coming = lax.ppermute(held, "dp", right) if step < size - 1 else None
+        update = jnp.einsum(
+            "tf,td->fd",
+            held,
+            lax.dynamic_slice_in_dim(columns, (index - step) % size * rows, held.shape[0], axis=0),
+            preferred_element_type=jnp.float32,
+        )
+        total_2 = update if total_2 is None else total_2 + update
+        held = coming
+    total = total_2
     down_grad = (total * scale).astype(jnp.bfloat16)
     return (gate_grad[None], up_grad[None], down_grad)
 

time: 348 us -> 384 us (1.10)
  blocking collectives: 122 us -> 0 us
  waiting for transfers between devices: 137 us -> 258 us
  matrix products: 58.4 us -> 88.3 us
  starting transfers between devices: 0.08 us -> 5.12 us
    ppermute x0 -> x3, waiting for transfers between devices: none -> 141 us  [on_device(): coming = lax.ppermute(held, 'dp', right) if step < size - 1 else None]
    all_to_all x1 -> x0, blocking collectives: 122 us -> none  [on_device(): lax.all_to_all(block, 'dp', split_axis=1, concat_axis=0, tiled=True)]
    all_gather x1 -> x0, waiting for transfers between devices: 33.6 us -> none  [on_device(): hidden_all = lax.all_gather(hidden, 'dp', axis=0, tiled=True)]
    dot_general x1 -> x4, matrix products: 25 us -> 55.3 us  [on_device(): jnp.einsum('tf,td->fd', held, lax.dynamic_slice_in_dim(columns, (index -...]
    all_to_all x0 -> x1, waiting for transfers between devices: none -> 14 us  [on_device(): lax.all_to_all(block, 'dp', split_axis=1, concat_axis=0, tiled=True)]
    all_to_all x0 -> x1, starting transfers between devices: none -> 5.07 us  [on_device(): lax.all_to_all(block, 'dp', split_axis=1, concat_axis=0, tiled=True)]
  transfers between devices with their start and end apart: 2 -> 5, of which waited for: 2 -> 5; matrix products, arithmetic and copies ran while one was open for 5% -> 13% of each run, Pallas kernels for 0% -> 0%
where the time goes in v1:
time: 384 us; the launch traced here: 383 us
  waiting for transfers between devices  258 us (67%)
  matrix products  88.3 us (23%)
  local copies, waits for them, and re-layouts  17.9 us (5%)
  between operations  14 us (4%)
  starting transfers between devices  5.12 us (1%)
    ppermute x3, waiting for transfers between devices, on_device(): coming = lax.ppermute(held, 'dp', right) if step < size - 1 else None  141 us
    all_gather x1, waiting for transfers between devices, on_device(): block = lax.all_gather(out_grad, 'tensor', axis=1, tiled=True)[0]  102 us
    dot_general x4, matrix products, on_device(): jnp.einsum('tf,td->fd', held, lax.dynamic_slice_in_dim(columns, (index -...  55.3 us
    dot_general x1, matrix products, on_device(): lax.dot_general(block, down_weight, (((1,), (1,)), ((), ())), preferred_e...  33 us
    all_to_all x1, waiting for transfers between devices, on_device(): lax.all_to_all(block, 'dp', split_axis=1, concat_axis=0, tiled=True)  14 us
    all_to_all x1, local copies, waits for them, and re-layouts, on_device(): lax.all_to_all(block, 'dp', split_axis=1, concat_axis=0, tiled=True)  7.85 us
    all_gather x1, local copies, waits for them, and re-layouts, on_device(): block = lax.all_gather(out_grad, 'tensor', axis=1, tiled=True)[0]  7.84 us
  transfers between devices with their start and end apart: 5, of which 5 were waited for; matrix products, arithmetic and copies ran while one was open for 13% of the time, Pallas kernels for 0%

profile of v1, /device:TPU:0, one launch (start us, length us, event | category | flops | bytes accessed | tf_op | source)
XLA Modules:
  0.0 383.1 jit_solution(3805921569988964307)
XLA Ops:
  7.2 0.0 all-gather.2.cloned.1.call-start
  7.2 0.7 all-gather.2.cloned.1.call-update
  7.9 102.5 %all-gather.2.cloned.1.call-done = bf16[1,640,4096]{2,1,0:T(8,128)(2,1)} async-done(((bf16[1,160,4096]{2,1,0:T(8,128)(2,1)}), bf16[1,640,4096]{2,1,0:T(8,128)(2,1)}) %all-gather.2.cloned.1.call-update) | async-done | bytes 5242896 | tf_op jit(solution)/shard_map/all_gather | solution.py:15
  110.4 33.0 %fusion.10 = (bf16[1,640,3584]{2,1,0:T(8,128)(2,1)}, bf16[1,640,3584]{2,1,0:T(8,128)(2,1)}, bf16[640,3584]{1,0:T(8,128)(2,1)S(1)}) fusion(bf16[1,640,3584]{2,1,0:T(8,128)(2,1)} %param.5, bf16[1,640,3584]{2,1,0:T(8,128)(2,1)} %param.6, bf16[3584,4096]{1,0:T(8,128)(2,1)} %param.7, bf16[1,640,4096]{2,1,0:T(8,128)(2,1)} %all-gather.2.cloned.1.call-done), kind=kOutput, calls=%fused_computation.17 | convolution fusion | flops 18829475840 | bytes 57540608 | tf_op jit(solution)/shard_map/dot_general | solution.py:17
  143.3 0.0 copy-start.1
  143.3 2.2 copy-done.1
  145.5 0.0 collective-permute-start
  145.5 52.2 %collective-permute-done = bf16[640,3584]{1,0:T(8,128)(2,1)} collective-permute-done((bf16[640,3584]{1,0:T(8,128)(2,1)S(1)}, bf16[640,3584]{1,0:T(8,128)(2,1)}, u32[]{:S(2)}, u32[]{:S(2)}) %collective-permute-start) | collective-permute-done | bytes 4587552 | tf_op jit(solution)/shard_map/ppermute | solution.py:26
  197.8 0.0 collective-permute-start.1
  197.8 7.8 %copy.9 = bf16[1,640,4096]{1,2,0:T(8,128)(2,1)} copy(bf16[1,640,4096]{2,1,0:T(8,128)(2,1)} %all-gather.2.cloned.1.call-done) | data formatting | bytes 10485760 | tf_op jit(solution)/shard_map/all_gather | solution.py:15
  205.6 5.1 %all-to-all-start = ((bf16[640,4,1024]{0,2,1:T(8,128)(2,1)}), bf16[640,4,1024]{0,2,1:T(8,128)(2,1)}, u32[]{:S(2)}, u32[]{:S(2)}) async-start(bf16[640,4,1024]{0,2,1:T(8,128)(2,1)} %bitcast.33), calls=%async_computation | async-start | bytes 10485760 | tf_op jit(solution)/shard_map/all_to_all | solution.py:16
  210.7 67.6 %collective-permute-done.1 = bf16[640,3584]{1,0:T(8,128)(2,1)} collective-permute-done((bf16[640,3584]{1,0:T(8,128)(2,1)}, bf16[640,3584]{1,0:T(8,128)(2,1)}, u32[]{:S(2)}, u32[]{:S(2)}) %collective-permute-start.1) | collective-permute-done | bytes 4587552 | tf_op jit(solution)/shard_map/ppermute | solution.py:26
  278.3 0.0 collective-permute-start.2
  278.3 14.0 %all-to-all-done = bf16[640,4,1024]{0,2,1:T(8,128)(2,1)} async-done(((bf16[640,4,1024]{0,2,1:T(8,128)(2,1)}), bf16[640,4,1024]{0,2,1:T(8,128)(2,1)}, u32[]{:S(2)}, u32[]{:S(2)}) %all-to-all-start) | async-done | bytes 5242912 | tf_op jit(solution)/shard_map/all_to_all | solution.py:16
  292.4 7.9 %copy.10 = bf16[4,640,1024]{2,1,0:T(8,128)(2,1)} copy(bf16[4,640,1024]{1,2,0:T(8,128)(2,1)} %bitcast.8) | data formatting | bytes 10485760 | tf_op jit(solution)/shard_map/all_to_all | solution.py:16
  300.2 0.0 copy-start
  300.2 11.8 %fusion.17 = f32[3584,1024]{1,0:T(8,128)} fusion(bf16[640,3584]{1,0:T(8,128)(2,1)} %copy-done.1, bf16[2560,1024]{1,0:T(8,128)(2,1)} %bitcast.34, s32[]{:T(128)S(6)} %select_n.32), kind=kOutput, calls=%fused_computation.24 | convolution fusion | flops 4697620480 | bytes 20578308 | tf_op jit(solution)/shard_map/tf,td->fd/dot_general | solution.py:27
  312.0 0.0 copy-done
  312.0 11.4 %fusion.15 = f32[3584,1024]{1,0:T(8,128)} fusion(bf16[640,3584]{1,0:T(8,128)(2,1)} %collective-permute-done, bf16[2560,1024]{1,0:T(8,128)(2,1)S(1)} %bitcast.35, s32[]{:T(128)S(6)} %select_n.34), kind=kOutput, calls=%fused_computation.22 | convolution fusion | flops 4697620480 | bytes 20578308 | tf_op jit(solution)/shard_map/tf,td->fd/dot_general | solution.py:27
  323.4 11.5 %fusion.13 = f32[3584,1024]{1,0:T(8,128)} fusion(bf16[640,3584]{1,0:T(8,128)(2,1)} %collective-permute-done.1, bf16[2560,1024]{1,0:T(8,128)(2,1)S(1)} %bitcast.36, s32[]{:T(128)S(6)} %select_n.36), kind=kOutput, calls=%fused_computation.20 | convolution fusion | flops 4697620480 | bytes 20578308 | tf_op jit(solution)/shard_map/tf,td->fd/dot_general | solution.py:27
  334.9 20.7 %collective-permute-done.2 = bf16[640,3584]{1,0:T(8,128)(2,1)} collective-permute-done((bf16[640,3584]{1,0:T(8,128)(2,1)}, bf16[640,3584]{1,0:T(8,128)(2,1)}, u32[]{:S(2)}, u32[]{:S(2)}) %collective-permute-start.2) | collective-permute-done | bytes 4587552 | tf_op jit(solution)/shard_map/ppermute | solution.py:26
  355.6 20.7 %multiply_convert_fusion = bf16[3584,1024]{1,0:T(8,128)(2,1)} fusion(f32[3584,1024]{1,0:T(8,128)} %fusion.13, f32[3584,1024]{1,0:T(8,128)} %fusion.17, f32[3584,1024]{1,0:T(8,128)} %fusion.15, bf16[640,3584]{1,0:T(8,128)(2,1)} %collective-permute-done.2, bf16[2560,1024]{1,0:T(8,128)(2,1)S(1)} %bitcast.37, s32[]{:T(128)S(6)} %select_n.38), kind=kOutput, calls=%fused_computation | convolution fusion | flops 4715970560 | bytes 57278468 | tf_op jit(solution)/shard_map/tf,td->fd/dot_general | solution.py:27
Async XLA Ops:
  7.2 103.2 %all-gather.2.cloned.1.call-start = ((), (), s32[]{:S(2)}) async-start(), calls=%async_computation.1 | async-start | bytes 6553600 | tf_op jit(solution)/shard_map/all_gather | solution.py:15
  143.3 2.2 copy-start.1
  145.5 52.2 %collective-permute-start = (bf16[640,3584]{1,0:T(8,128)(2,1)S(1)}, bf16[640,3584]{1,0:T(8,128)(2,1)}, u32[]{:S(2)}, u32[]{:S(2)}) collective-permute-start(bf16[640,3584]{1,0:T(8,128)(2,1)S(1)} %get-tuple-element.5), channel_id=1, source_target_pairs={{0,1},{1,2},{2,3},{3,0},{4,5},{5,6},{6,7},{7,4},{8,9},{9,10},{10,1... | collective-permute-start | bytes 13762568 | tf_op jit(solution)/shard_map/ppermute | solution.py:26
  197.8 80.5 %collective-permute-start.1 = (bf16[640,3584]{1,0:T(8,128)(2,1)}, bf16[640,3584]{1,0:T(8,128)(2,1)}, u32[]{:S(2)}, u32[]{:S(2)}) collective-permute-start(bf16[640,3584]{1,0:T(8,128)(2,1)} %collective-permute-done), channel_id=1, source_target_pairs={{0,1},{1,2},{2,3},{3,0},{4,5},{5,6},{6,7},{7,4},{8,9},{9,10},{10,1... | collective-permute-start | bytes 13762568 | tf_op jit(solution)/shard_map/ppermute | solution.py:26
  205.6 86.8 %all-to-all-start = ((bf16[640,4,1024]{0,2,1:T(8,128)(2,1)}), bf16[640,4,1024]{0,2,1:T(8,128)(2,1)}, u32[]{:S(2)}, u32[]{:S(2)}) async-start(bf16[640,4,1024]{0,2,1:T(8,128)(2,1)} %bitcast.33), calls=%async_computation | async-start | bytes 10485760 | tf_op jit(solution)/shard_map/all_to_all | solution.py:16
  278.3 77.2 %collective-permute-start.2 = (bf16[640,3584]{1,0:T(8,128)(2,1)}, bf16[640,3584]{1,0:T(8,128)(2,1)}, u32[]{:S(2)}, u32[]{:S(2)}) collective-permute-start(bf16[640,3584]{1,0:T(8,128)(2,1)} %collective-permute-done.1), channel_id=1, source_target_pairs={{0,1},{1,2},{2,3},{3,0},{4,5},{5,6},{6,7},{7,4},{8,9},{9,10},{10,1... | collective-permute-start | bytes 13762568 | tf_op jit(solution)/shard_map/ppermute | solution.py:26
  300.2 11.8 %copy-start = (bf16[4,640,1024]{2,1,0:T(8,128)(2,1)S(1)}, bf16[4,640,1024]{2,1,0:T(8,128)(2,1)}, u32[]{:S(2)}) copy-start(bf16[4,640,1024]{2,1,0:T(8,128)(2,1)} %copy.10) | copy-start | bytes 15728644
Sparse Core Ops, SparseCore 0:
  9.6 100.7 all-gather.1
